TPU v7x, 128 devices: a whole 4x4x4 slice. The times are simulated.
128 devices in a mesh: dom: 128 (over x, y, z, core).
Axes of the slice: x: 4, y: 4, z: 4, core: 2. Of those that a mesh axis runs over, the one named last changes fastest.
Arguments:
- state: float32 [9, 56, 49152], P(None, None, 'dom'), may hold values from -18 to 18
- class_label: int32 [49152], P('dom'), may hold values from 0 to 2, as said below
- stiffness: float32 [3, 56, 56], replicated, may hold values from -0.8 to 0.8
- star: float32 [3, 9, 9, 49152], P(None, None, None, 'dom'), may hold values from -0.84 to 0.84
- face_proj: float32 [4, 21, 56], replicated, may hold values from -0.75 to 0.75
- orient_map: float32 [3, 21, 21], replicated, may hold values from -1.25 to 1.25
- flux_local: float32 [4, 9, 9, 49152], P(None, None, None, 'dom'), may hold values from -0.12 to 0.15
- flux_neigh: float32 [4, 9, 9, 49152], P(None, None, None, 'dom'), may hold values from -0.12 to 0.12
- neighbor: int32 [4, 49152], P(None, 'dom'), may hold values from 0 to 1151, as said below
- neighbor_face: int32 [4, 49152], P(None, 'dom'), may hold values from 0 to 3
- orientation: int32 [4, 49152], P(None, 'dom'), may hold values from 0 to 2
- send_list: int32 [3072, 32], P('dom'), may hold values from -1 to 383, as said below
Outputs:
- final_state: float32 [9, 56, 49152], P(None, None, 'dom')
- energy: float32 [1], replicated
Inputs may be any that keep to these rules, and one draw needn't show every extreme that they name: `class_label`: each device's block of 384 elements holds exactly 128 elements of each class 0, 1 and 2. `send_list`: row 3 (2 * 4 d + p) + g lists the local elements of device d sent to its bordering partition p for that partition's elements of class g: distinct indices followed by -1 for unused slots, at least one slot used; every device receives one row with all 32 slots used. `neighbor`: A value under 384 is another element of the same device; a value 384 + (3 p + g) * 32 + r names slot r of the row that bordering partition p sends for class g, stands only on faces of class-g elements, always names a used slot, and every used slot is named by exactly one face.
All inputs are finite; a program needn't handle non-finite values.
Results may differ from a plain program's by a relative error of at most 0.0001.
Values sent between devices are 32-bit elements; how exact they have to be, the bound alone decides.
No kernel may reach another device: no remote copies, remote signals or barrier semaphores. Data moves between devices by JAX's collectives and lax.ppermute only.
A program may use at most 256 MiB of HBM per device.

v0:
```python
import math
import jax
import jax.numpy as jnp
from jax import lax
from jax.sharding import PartitionSpec as P

ORDER = 6
CYCLES = 1
HIGH = lax.Precision.HIGHEST


def from_behind(block, axis, distance):
    devices = range(lax.axis_size(axis))
    route = [((i - distance) % len(devices), i) for i in devices]
    return lax.ppermute(block, axis, route)


def element_mix(matrix, values):
    total = None
    for q in range(matrix.shape[1]):
        term = matrix[:, q, None, :] * values[q][None, :, :]
        total = term if total is None else total + term
    return total


def apply_star(values, stiffness, star):
    total = None
    for d in range(3):
        moved = jnp.einsum("ab,qbe->qae", stiffness[d], values, precision=HIGH)
        term = element_mix(star[d], moved)
        total = term if total is None else total + term
    return total


def predict(values, stiffness, star):
    derivs = [values]
    for k in range(ORDER - 1):
        derivs.append(apply_star(derivs[-1], stiffness, star))
    return derivs


def integrate(derivs, start):
    total = None
    for k in range(ORDER):
        weight = ((start + 1.0) ** (k + 1) - float(start) ** (k + 1)) / math.factorial(k + 1)
        term = derivs[k] * weight
        total = term if total is None else total + term
    return total


def correct(
    values,
    own,
    near,
    near_face,
    near_orient,
    stiffness,
    star,
    face_proj,
    orient_map,
    flux_local,
    flux_neigh,
):
    update = apply_star(own, stiffness, star)
    for f in range(4):
        on_face = jnp.einsum("ab,qbe->qae", face_proj[f], own, precision=HIGH)
        lifted = jnp.einsum("ba,qbe->qae", face_proj[f], on_face, precision=HIGH)
        update = update - element_mix(flux_local[f], lifted)
        chosen = None
        for j in range(4):
            projected = jnp.einsum("ab,qbe->qae", face_proj[j], near[:, :, f, :], precision=HIGH)
            term = jnp.where((near_face[f] == j)[None, None, :], projected, 0.0)
            chosen = term if chosen is None else chosen + term
        aligned = None
        for h in range(3):
            turned = jnp.einsum("ab,qbe->qae", orient_map[h], chosen, precision=HIGH)
            term = jnp.where((near_orient[f] == h)[None, None, :], turned, 0.0)
            aligned = term if aligned is None else aligned + term
        lifted_near = jnp.einsum("ba,qbe->qae", face_proj[f], aligned, precision=HIGH)
        update = update - element_mix(flux_neigh[f], lifted_near)
    return values + update


def shards(
    state,
    class_label,
    stiffness,
    star,
    face_proj,
    orient_map,
    flux_local,
    flux_neigh,
    neighbor,
    neighbor_face,
    orientation,
    send_list,
):
    quant_count = state.shape[0]
    basis_count = state.shape[1]
    elements = state.shape[2]
    per_class = elements // 3
    devices = lax.axis_size("dom")
    row_count = send_list.shape[0]
    peer_count = row_count // 3
    slot_count = send_list.shape[1]
    reach_count = peer_count // 2
    ghost_count = row_count * slot_count
    offsets = [
        p - reach_count if p < reach_count else p - reach_count + 1 for p in range(peer_count)
    ]
    class_order = jnp.argsort(class_label, stable=True)
    rank_of = jnp.argsort(class_order)
    extended_rank = jnp.concatenate([rank_of, elements + jnp.arange(ghost_count, dtype=jnp.int32)])
    near_index = jnp.take(extended_rank, neighbor[:, class_order].reshape(-1), axis=0)
    near_face = neighbor_face[:, class_order]
    near_orient = orientation[:, class_order]
    star_sorted = star[:, :, :, class_order]
    local_sorted = flux_local[:, :, :, class_order]
    neigh_sorted = flux_neigh[:, :, :, class_order]
    send_flat = send_list.reshape(-1)
    send_sorted = jnp.take(rank_of, jnp.maximum(send_flat, 0), axis=0)
    send_valid = (send_flat >= 0).astype(jnp.float32)
    sorted_state = state[:, :, class_order]
    fields = [sorted_state[:, :, c * per_class : (c + 1) * per_class] for c in range(3)]
    derivs = [None, None, None]
    owns = [None, None, None]
    nears = [None, None, None]
    energies = []
    for n in range(4 * CYCLES):
        pieces = []
        for c in range(3):
            span = 2**c
            window = slice(c * per_class, (c + 1) * per_class)
            if n % span == 0:
                derivs[c] = predict(fields[c], stiffness, star_sorted[:, :, :, window])
            pieces.append(integrate(derivs[c], n % span))
        current = jnp.concatenate(pieces, axis=2)
        outgoing = (jnp.take(current, send_sorted, axis=2) * send_valid).reshape(
            quant_count, basis_count, peer_count, 3, slot_count
        )
        outbound = jnp.transpose(
            outgoing.reshape(quant_count, basis_count, peer_count, 3 * slot_count), (2, 0, 1, 3)
        )
        outbound = outbound.reshape(peer_count, quant_count, basis_count * 3 * slot_count)
        received = []
        for p in range(peer_count):
            arrived = from_behind(outbound[peer_count - 1 - p], "dom", -offsets[p])
            received.append(arrived.reshape(quant_count, basis_count, 3 * slot_count))
        ghost_values = jnp.concatenate(received, axis=2)
        extended = jnp.concatenate([current, ghost_values], axis=2)
        gathered = jnp.take(extended, near_index, axis=2).reshape(
            quant_count, basis_count, 4, elements
        )
        for c in range(3):
            span = 2**c
            window = slice(c * per_class, (c + 1) * per_class)
            if n % span == 0:
                owns[c] = pieces[c]
                nears[c] = gathered[:, :, :, window]
            else:
                owns[c] = owns[c] + pieces[c]
                nears[c] = nears[c] + gathered[:, :, :, window]
            if (n + 1) % span == 0:
                fields[c] = correct(
                    fields[c],
                    owns[c],
                    nears[c],
                    near_face[:, window],
                    near_orient[:, window],
                    stiffness,
                    star_sorted[:, :, :, window],
                    face_proj,
                    orient_map,
                    local_sorted[:, :, :, window],
                    neigh_sorted[:, :, :, window],
                )
        if (n + 1) % 4 == 0:
            energies.append(
                jnp.sum(fields[0] * fields[0])
                + jnp.sum(fields[1] * fields[1])
                + jnp.sum(fields[2] * fields[2])
            )
    totals = lax.psum(jnp.stack(energies), "dom")
    energy = totals / (devices * elements * quant_count * basis_count)
    final_sorted = jnp.concatenate(fields, axis=2)
    final_state = jnp.take(final_sorted, rank_of, axis=2)
    return (final_state, energy)


def solution(mesh):
    in_specs = (
        P(None, None, "dom"),
        P("dom"),
        P(),
        P(None, None, None, "dom"),
        P(),
        P(),
        P(None, None, None, "dom"),
        P(None, None, None, "dom"),
        P(None, "dom"),
        P(None, "dom"),
        P(None, "dom"),
        P("dom", None),
    )
    out_specs = (P(None, None, "dom"), P())
    return jax.shard_map(shards, mesh=mesh, in_specs=in_specs, out_specs=out_specs, check_vma=False)
```

profile of v0, /device:TPU:3, one launch (start us, length us, event | category | flops | bytes accessed | tf_op | source)
XLA Modules:
  0.0 1443.8 jit_solution(17035889397841479485)
XLA Ops:
  31.8 11.5 gather_fusion.1
  43.4 14.6 %fusion.702 = (f32[1,9,9,128]{2,0,1,3:T(1,128)S(1)}, f32[1,9,9,128]{2,0,1,3:T(1,128)S(1)}, f32[1,9,9,128]{2,0,1,3:T(1,128)}, f32[1,9,9,128]{2,0,1,3:T(1,128)}, f...) fusion(f32[3,9,9,384]{2,0,1,3:T(4,128)} %bitcast.5746), kind=kLoop, calls=%fused_computation.3250 | loop fusion | bytes 746496 | tf_op jit(solution)/shard_map/slice | solution.py:30
  262.7 8.8 gather_fusion.8
  311.9 11.5 gather_fusion.2
  323.4 15.9 %fusion.700 = (f32[1,9,9,128]{2,0,1,3:T(1,128)}, f32[1,9,9,128]{2,0,1,3:T(1,128)}, f32[1,9,9,128]{2,0,1,3:T(1,128)}, f32[1,9,9,128]{2,0,1,3:T(1,128)}, f32[1,9,9...) fusion(f32[4,9,9,384]{2,0,1,3:T(4,128)} %bitcast.5721), kind=kLoop, calls=%fused_computation.3248 | loop fusion | bytes 995328 | tf_op jit(solution)/shard_map/slice | solution.py:68
  383.9 11.5 gather_fusion.3
  395.4 16.2 %fusion.701 = (f32[1,9,9,128]{2,0,1,3:T(1,128)}, f32[1,9,9,128]{2,0,1,3:T(1,128)}, f32[1,9,9,128]{2,0,1,3:T(1,128)}, f32[1,9,9,128]{2,0,1,3:T(1,128)}, f32[1,9,9...) fusion(f32[4,9,9,384]{2,0,1,3:T(4,128)} %bitcast.5720), kind=kLoop, calls=%fused_computation.3249 | loop fusion | bytes 995328 | tf_op jit(solution)/shard_map/slice | solution.py:80
  601.9 12.2 gather_fusion.11
  614.1 9.6 broadcast_select_fusion.3
  744.4 8.9 collective-permute-done.9
  781.5 8.2 copy.453
  789.8 12.2 gather_fusion.13
  802.0 9.8 broadcast_select_fusion.2
  993.3 12.6 collective-permute-start.17
  1013.9 7.6 collective-permute-done.17
  1045.6 8.2 copy.478
  1053.8 12.2 gather_fusion.15
  1066.0 9.6 broadcast_select_fusion.1
  1185.1 8.9 collective-permute-start.25
  1201.3 8.1 collective-permute-done.25
  1233.5 8.2 copy.493
  1241.7 12.2 gather_fusion.17
  1253.9 9.4 broadcast_select_fusion
  1353.8 74.4 %psum.7 = f32[1]{0:T(128)} all-reduce(f32[1]{0:T(128)} %bitcast.2021), channel_id=1, replica_groups=mesh['dom'=128] {'dom'}, use_global_device_ids=true, to_apply=%region_5.8 | all-reduce | flops 1 | bytes 8 | tf_op jit(solution)/shard_map/psum | solution.py:183
  (2061 shorter events, 1106.4 us)
Async XLA Ops:
  205.8 355.6 %collective-permute-start = (f32[9,5376]{1,0:T(8,128)}, f32[9,5376]{1,0:T(8,128)}, u32[]{:S(2)}, u32[]{:S(2)}) collective-permute-start(f32[9,5376]{1,0:T(8,128)} %squeeze.221), channel_id=1, source_target_pairs={{124,0},{125,1},{126,2},{127,3},{0,4},{1,5},{2,6},{3,7},{4,8},{5,9... | collective-permute-start | bytes 580616 | tf_op jit(solution)/shard_map/ppermute | solution.py:15
  213.2 352.3 %collective-permute-start.1 = (f32[9,5376]{1,0:T(8,128)}, f32[9,5376]{1,0:T(8,128)}, u32[]{:S(2)}, u32[]{:S(2)}) collective-permute-start(f32[9,5376]{1,0:T(8,128)} %squeeze.222), channel_id=1, source_target_pairs={{125,0},{126,1},{127,2},{0,3},{1,4},{2,5},{3,6},{4,7},{5,8},{6,9},... | collective-permute-start | bytes 580616 | tf_op jit(solution)/shard_map/ppermute | solution.py:15
  218.3 349.4 %collective-permute-start.2 = (f32[9,5376]{1,0:T(8,128)}, f32[9,5376]{1,0:T(8,128)}, u32[]{:S(2)}, u32[]{:S(2)}) collective-permute-start(f32[9,5376]{1,0:T(8,128)} %squeeze.223), channel_id=1, source_target_pairs={{126,0},{127,1},{0,2},{1,3},{2,4},{3,5},{4,6},{5,7},{6,8},{7,9},{8... | collective-permute-start | bytes 580616 | tf_op jit(solution)/shard_map/ppermute | solution.py:15
  223.8 351.9 %collective-permute-start.3 = (f32[9,5376]{1,0:T(8,128)}, f32[9,5376]{1,0:T(8,128)}, u32[]{:S(2)}, u32[]{:S(2)}) collective-permute-start(f32[9,5376]{1,0:T(8,128)} %squeeze.224), channel_id=1, source_target_pairs={{127,0},{0,1},{1,2},{2,3},{3,4},{4,5},{5,6},{6,7},{7,8},{8,9},{9,1... | collective-permute-start | bytes 580616 | tf_op jit(solution)/shard_map/ppermute | solution.py:15
  227.7 349.9 %collective-permute-start.4 = (f32[9,5376]{1,0:T(8,128)}, f32[9,5376]{1,0:T(8,128)}, u32[]{:S(2)}, u32[]{:S(2)}) collective-permute-start(f32[9,5376]{1,0:T(8,128)} %squeeze.225), channel_id=1, source_target_pairs={{1,0},{2,1},{3,2},{4,3},{5,4},{6,5},{7,6},{8,7},{9,8},{10,9},{11,1... | collective-permute-start | bytes 580616 | tf_op jit(solution)/shard_map/ppermute | solution.py:15
  561.4 18.0 %collective-permute-start.5 = (f32[9,5376]{1,0:T(8,128)}, f32[9,5376]{1,0:T(8,128)S(1)}, u32[]{:S(2)}, u32[]{:S(2)}) collective-permute-start(f32[9,5376]{1,0:T(8,128)} %squeeze.226), channel_id=1, source_target_pairs={{2,0},{3,1},{4,2},{5,3},{6,4},{7,5},{8,6},{9,7},{10,8},{11,9},{12,... | collective-permute-start | bytes 580616 | tf_op jit(solution)/shard_map/ppermute | solution.py:15
  565.5 18.0 %collective-permute-start.6 = (f32[9,5376]{1,0:T(8,128)}, f32[9,5376]{1,0:T(8,128)S(1)}, u32[]{:S(2)}, u32[]{:S(2)}) collective-permute-start(f32[9,5376]{1,0:T(8,128)} %squeeze.227), channel_id=1, source_target_pairs={{3,0},{4,1},{5,2},{6,3},{7,4},{8,5},{9,6},{10,7},{11,8},{12,9},{13... | collective-permute-start | bytes 580616 | tf_op jit(solution)/shard_map/ppermute | solution.py:15
  567.7 23.1 %collective-permute-start.7 = (f32[9,5376]{1,0:T(8,128)S(1)}, f32[9,5376]{1,0:T(8,128)S(1)}, u32[]{:S(2)}, u32[]{:S(2)}) collective-permute-start(f32[9,5376]{1,0:T(8,128)S(1)} %copy-done.113), channel_id=1, source_target_pairs={{4,0},{5,1},{6,2},{7,3},{8,4},{9,5},{10,6},{11,7},{12,8},{13,9},{1... | collective-permute-start | bytes 580616 | tf_op jit(solution)/shard_map/ppermute | solution.py:15
  734.2 19.1 %collective-permute-start.9 = (f32[9,5376]{1,0:T(8,128)}, f32[9,5376]{1,0:T(8,128)S(1)}, u32[]{:S(2)}, u32[]{:S(2)}) collective-permute-start(f32[9,5376]{1,0:T(8,128)} %squeeze.246), channel_id=1, source_target_pairs={{125,0},{126,1},{127,2},{0,3},{1,4},{2,5},{3,6},{4,7},{5,8},{6,9},... | collective-permute-start | bytes 580616 | tf_op jit(solution)/shard_map/ppermute | solution.py:15
  736.3 19.9 %collective-permute-start.10 = (f32[9,5376]{1,0:T(8,128)}, f32[9,5376]{1,0:T(8,128)S(1)}, u32[]{:S(2)}, u32[]{:S(2)}) collective-permute-start(f32[9,5376]{1,0:T(8,128)} %squeeze.247), channel_id=1, source_target_pairs={{126,0},{127,1},{0,2},{1,3},{2,4},{3,5},{4,6},{5,7},{6,8},{7,9},{8... | collective-permute-start | bytes 580616 | tf_op jit(solution)/shard_map/ppermute | solution.py:15
  736.3 31.9 %collective-permute-start.11 = (f32[9,5376]{1,0:T(8,128)}, f32[9,5376]{1,0:T(8,128)}, u32[]{:S(2)}, u32[]{:S(2)}) collective-permute-start(f32[9,5376]{1,0:T(8,128)} %squeeze.248), channel_id=1, source_target_pairs={{127,0},{0,1},{1,2},{2,3},{3,4},{4,5},{5,6},{6,7},{7,8},{8,9},{9,1... | collective-permute-start | bytes 580616 | tf_op jit(solution)/shard_map/ppermute | solution.py:15
  736.3 33.8 %collective-permute-start.12 = (f32[9,5376]{1,0:T(8,128)}, f32[9,5376]{1,0:T(8,128)}, u32[]{:S(2)}, u32[]{:S(2)}) collective-permute-start(f32[9,5376]{1,0:T(8,128)} %squeeze.249), channel_id=1, source_target_pairs={{1,0},{2,1},{3,2},{4,3},{5,4},{6,5},{7,6},{8,7},{9,8},{10,9},{11,1... | collective-permute-start | bytes 580616 | tf_op jit(solution)/shard_map/ppermute | solution.py:15
  741.3 30.6 %collective-permute-start.13 = (f32[9,5376]{1,0:T(8,128)}, f32[9,5376]{1,0:T(8,128)}, u32[]{:S(2)}, u32[]{:S(2)}) collective-permute-start(f32[9,5376]{1,0:T(8,128)} %squeeze.250), channel_id=1, source_target_pairs={{2,0},{3,1},{4,2},{5,3},{6,4},{7,5},{8,6},{9,7},{10,8},{11,9},{12,... | collective-permute-start | bytes 580616 | tf_op jit(solution)/shard_map/ppermute | solution.py:15
  753.3 20.4 %collective-permute-start.14 = (f32[9,5376]{1,0:T(8,128)}, f32[9,5376]{1,0:T(8,128)}, u32[]{:S(2)}, u32[]{:S(2)}) collective-permute-start(f32[9,5376]{1,0:T(8,128)} %squeeze.251), channel_id=1, source_target_pairs={{3,0},{4,1},{5,2},{6,3},{7,4},{8,5},{9,6},{10,7},{11,8},{12,9},{13... | collective-permute-start | bytes 580616 | tf_op jit(solution)/shard_map/ppermute | solution.py:15
  756.3 19.3 %collective-permute-start.15 = (f32[9,5376]{1,0:T(8,128)}, f32[9,5376]{1,0:T(8,128)}, u32[]{:S(2)}, u32[]{:S(2)}) collective-permute-start(f32[9,5376]{1,0:T(8,128)} %squeeze.252), channel_id=1, source_target_pairs={{4,0},{5,1},{6,2},{7,3},{8,4},{9,5},{10,6},{11,7},{12,8},{13,9},{1... | collective-permute-start | bytes 580616 | tf_op jit(solution)/shard_map/ppermute | solution.py:15
  993.3 28.1 %collective-permute-start.17 = (f32[9,5376]{1,0:T(8,128)}, f32[9,5376]{1,0:T(8,128)S(1)}, u32[]{:S(2)}, u32[]{:S(2)}) collective-permute-start(f32[9,5376]{1,0:T(8,128)} %squeeze.270), channel_id=1, source_target_pairs={{125,0},{126,1},{127,2},{0,3},{1,4},{2,5},{3,6},{4,7},{5,8},{6,9},... | collective-permute-start | bytes 580616 | tf_op jit(solution)/shard_map/ppermute | solution.py:15
  1006.0 20.3 %collective-permute-start.18 = (f32[9,5376]{1,0:T(8,128)}, f32[9,5376]{1,0:T(8,128)S(1)}, u32[]{:S(2)}, u32[]{:S(2)}) collective-permute-start(f32[9,5376]{1,0:T(8,128)} %squeeze.271), channel_id=1, source_target_pairs={{126,0},{127,1},{0,2},{1,3},{2,4},{3,5},{4,6},{5,7},{6,8},{7,9},{8... | collective-permute-start | bytes 580616 | tf_op jit(solution)/shard_map/ppermute | solution.py:15
  1006.1 25.8 %collective-permute-start.19 = (f32[9,5376]{1,0:T(8,128)}, f32[9,5376]{1,0:T(8,128)}, u32[]{:S(2)}, u32[]{:S(2)}) collective-permute-start(f32[9,5376]{1,0:T(8,128)} %squeeze.272), channel_id=1, source_target_pairs={{127,0},{0,1},{1,2},{2,3},{3,4},{4,5},{5,6},{6,7},{7,8},{8,9},{9,1... | collective-permute-start | bytes 580616 | tf_op jit(solution)/shard_map/ppermute | solution.py:15
  1006.1 27.6 %collective-permute-start.20 = (f32[9,5376]{1,0:T(8,128)}, f32[9,5376]{1,0:T(8,128)}, u32[]{:S(2)}, u32[]{:S(2)}) collective-permute-start(f32[9,5376]{1,0:T(8,128)} %squeeze.273), channel_id=1, source_target_pairs={{1,0},{2,1},{3,2},{4,3},{5,4},{6,5},{7,6},{8,7},{9,8},{10,9},{11,1... | collective-permute-start | bytes 580616 | tf_op jit(solution)/shard_map/ppermute | solution.py:15
  1008.2 27.3 %collective-permute-start.21 = (f32[9,5376]{1,0:T(8,128)}, f32[9,5376]{1,0:T(8,128)}, u32[]{:S(2)}, u32[]{:S(2)}) collective-permute-start(f32[9,5376]{1,0:T(8,128)} %squeeze.274), channel_id=1, source_target_pairs={{2,0},{3,1},{4,2},{5,3},{6,4},{7,5},{8,6},{9,7},{10,8},{11,9},{12,... | collective-permute-start | bytes 580616 | tf_op jit(solution)/shard_map/ppermute | solution.py:15
  1185.1 24.3 %collective-permute-start.25 = (f32[9,5376]{1,0:T(8,128)}, f32[9,5376]{1,0:T(8,128)S(1)}, u32[]{:S(2)}, u32[]{:S(2)}) collective-permute-start(f32[9,5376]{1,0:T(8,128)} %squeeze.282), channel_id=1, source_target_pairs={{125,0},{126,1},{127,2},{0,3},{1,4},{2,5},{3,6},{4,7},{5,8},{6,9},... | collective-permute-start | bytes 580616 | tf_op jit(solution)/shard_map/ppermute | solution.py:15
  1194.1 26.3 %collective-permute-start.27 = (f32[9,5376]{1,0:T(8,128)}, f32[9,5376]{1,0:T(8,128)}, u32[]{:S(2)}, u32[]{:S(2)}) collective-permute-start(f32[9,5376]{1,0:T(8,128)} %squeeze.284), channel_id=1, source_target_pairs={{127,0},{0,1},{1,2},{2,3},{3,4},{4,5},{5,6},{6,7},{7,8},{8,9},{9,1... | collective-permute-start | bytes 580616 | tf_op jit(solution)/shard_map/ppermute | solution.py:15
  1194.3 28.0 %collective-permute-start.28 = (f32[9,5376]{1,0:T(8,128)}, f32[9,5376]{1,0:T(8,128)}, u32[]{:S(2)}, u32[]{:S(2)}) collective-permute-start(f32[9,5376]{1,0:T(8,128)} %squeeze.285), channel_id=1, source_target_pairs={{1,0},{2,1},{3,2},{4,3},{5,4},{6,5},{7,6},{8,7},{9,8},{10,9},{11,1... | collective-permute-start | bytes 580616 | tf_op jit(solution)/shard_map/ppermute | solution.py:15
  1195.8 28.2 %collective-permute-start.29 = (f32[9,5376]{1,0:T(8,128)}, f32[9,5376]{1,0:T(8,128)}, u32[]{:S(2)}, u32[]{:S(2)}) collective-permute-start(f32[9,5376]{1,0:T(8,128)} %squeeze.286), channel_id=1, source_target_pairs={{2,0},{3,1},{4,2},{5,3},{6,4},{7,5},{8,6},{9,7},{10,8},{11,9},{12,... | collective-permute-start | bytes 580616 | tf_op jit(solution)/shard_map/ppermute | solution.py:15
  (485 other events, 11725.3 us)
where the time goes:
time: 1470 us; the launch traced here: 1440 us
  local copies, waits for them, and re-layouts  786 us (53%)
  matrix products  239 us (16%)
  other arithmetic  208 us (14%)
  blocking collectives  74.4 us (5%)
  starting transfers between devices  70.3 us (5%)
  waiting for transfers between devices  50.5 us (3%)
  between operations  15 us (1%)
    unnamed x1137, local copies, waits for them, and re-layouts  223 us
    mul x179, local copies, waits for them, and re-layouts, element_mix(): term = matrix[:, q, None, :] * values[q][None, :, :]  82.7 us
    psum x1, blocking collectives, shards(): totals = lax.psum(jnp.stack(energies), 'dom')  74.4 us
    dot_general x126, matrix products, apply_star(): moved = jnp.einsum('ab,qbe->qae', stiffness[d], values, precision=HIGH)  71.5 us
    ppermute x32, starting transfers between devices, from_behind(): return lax.ppermute(block, axis, route)  70.3 us
    dot_general x112, matrix products, correct(): jnp.einsum('ab,qbe->qae', face_proj[j], near[:, :, f, :], precision=HIGH)  61.5 us
    slice x36, local copies, waits for them, and re-layouts, shards(): arrived = from_behind(outbound[peer_count - 1 - p], 'dom', -offsets[p])  54.1 us
    reshape x32, local copies, waits for them, and re-layouts, shards(): received.append(arrived.reshape(quant_count, basis_count, 3 * slot_count))  51.4 us
  transfers between devices with their start and end apart: 32, of which 13 were waited for; matrix products, arithmetic and copies ran while one was open for 28% of the time, Pallas kernels for 0%

commit v1 on v0

--- a/solution.py
+++ b/solution.py
@@ -180,7 +180,7 @@
                 + jnp.sum(fields[1] * fields[1])
                 + jnp.sum(fields[2] * fields[2])
             )
-    totals = lax.psum(jnp.stack(energies), "dom")
+    totals = jnp.sum(lax.all_gather(jnp.stack(energies), "dom"), axis=0)
     energy = totals / (devices * elements * quant_count * basis_count)
     final_sorted = jnp.concatenate(fields, axis=2)
     final_state = jnp.take(final_sorted, rank_of, axis=2)

time: 1470 us -> 1480 us (level)
    psum x1 -> x0, blocking collectives: 74.4 us -> none  [shards(): totals = lax.psum(jnp.stack(energies), 'dom')]
    unnamed x0 -> x1, blocking collectives: none -> 73.9 us
    unnamed x1137 -> x1109, local copies, waits for them, and re-layouts: 223 us -> 228 us
where the time goes in v1:
time: 1480 us; the launch traced here: 1450 us
  local copies, waits for them, and re-layouts  792 us (54%)
  matrix products  244 us (16%)
  other arithmetic  208 us (14%)
  blocking collectives  73.9 us (5%)
  starting transfers between devices  70.3 us (5%)
  waiting for transfers between devices  50.4 us (3%)
  between operations  14.8 us (1%)
    unnamed x1109, local copies, waits for them, and re-layouts  228 us
    mul x179, local copies, waits for them, and re-layouts, element_mix(): term = matrix[:, q, None, :] * values[q][None, :, :]  83.7 us
    unnamed x1, blocking collectives  73.9 us
    dot_general x126, matrix products, apply_star(): moved = jnp.einsum('ab,qbe->qae', stiffness[d], values, precision=HIGH)  73.1 us
    ppermute x32, starting transfers between devices, from_behind(): return lax.ppermute(block, axis, route)  70.3 us
    dot_general x112, matrix products, correct(): jnp.einsum('ab,qbe->qae', face_proj[j], near[:, :, f, :], precision=HIGH)  62.3 us
    slice x36, local copies, waits for them, and re-layouts, shards(): arrived = from_behind(outbound[peer_count - 1 - p], 'dom', -offsets[p])  54.3 us
    dot_general x84, matrix products, correct(): turned = jnp.einsum('ab,qbe->qae', orient_map[h], chosen, precision=HIGH)  52.5 us
  transfers between devices with their start and end apart: 32, of which 13 were waited for; matrix products, arithmetic and copies ran while one was open for 28% of the time, Pallas kernels for 0%

profile of v1, /device:TPU:3, one launch (start us, length us, event | category | flops | bytes accessed | tf_op | source)
XLA Modules:
  0.0 1452.8 jit_solution(3508705265567975231)
XLA Ops:
  33.2 11.5 gather_fusion.1
  44.8 14.4 fusion.702
  268.3 8.8 gather_fusion.8
  316.5 11.5 gather_fusion.2
  328.0 16.1 %fusion.700 = (f32[1,9,9,128]{2,0,1,3:T(1,128)}, f32[1,9,9,128]{2,0,1,3:T(1,128)}, f32[1,9,9,128]{2,0,1,3:T(1,128)}, f32[1,9,9,128]{2,0,1,3:T(1,128)}, f32[1,9,9...) fusion(f32[4,9,9,384]{2,0,1,3:T(4,128)} %bitcast.5722), kind=kLoop, calls=%fused_computation.3248 | loop fusion | bytes 995328 | tf_op jit(solution)/shard_map/slice | solution.py:68
  388.8 11.5 gather_fusion.3
  400.3 16.3 %fusion.701 = (f32[1,9,9,128]{2,0,1,3:T(1,128)}, f32[1,9,9,128]{2,0,1,3:T(1,128)}, f32[1,9,9,128]{2,0,1,3:T(1,128)}, f32[1,9,9,128]{2,0,1,3:T(1,128)}, f32[1,9,9...) fusion(f32[4,9,9,384]{2,0,1,3:T(4,128)} %bitcast.5721), kind=kLoop, calls=%fused_computation.3249 | loop fusion | bytes 995328 | tf_op jit(solution)/shard_map/slice | solution.py:80
  607.1 12.2 gather_fusion.11
  619.3 9.6 broadcast_select_fusion.3
  753.5 9.0 collective-permute-done.9
  790.7 8.2 copy.453
  799.0 12.2 gather_fusion.13
  811.2 9.8 broadcast_select_fusion.2
  1001.7 12.6 collective-permute-start.17
  1022.2 7.6 collective-permute-done.17
  1054.1 8.2 copy.478
  1062.3 12.2 gather_fusion.15
  1074.6 9.6 broadcast_select_fusion.1
  1194.4 8.8 collective-permute-start.25
  1210.4 8.1 collective-permute-done.25
  1242.4 8.2 copy.493
  1250.6 12.2 gather_fusion.17
  1262.8 9.4 broadcast_select_fusion
  1362.7 73.9 %all-reduce = f32[128]{0:T(128)S(1)} all-reduce(f32[128]{0:T(128)S(1)} %dynamic-update-slice), channel_id=1, replica_groups=mesh['dom'=128] {'dom'}, use_global_device_ids=true, to_apply=%add | all-reduce | flops 128 | bytes 1024
  (2034 shorter events, 1116.0 us)
Async XLA Ops:
  211.3 355.3 %collective-permute-start = (f32[9,5376]{1,0:T(8,128)}, f32[9,5376]{1,0:T(8,128)}, u32[]{:S(2)}, u32[]{:S(2)}) collective-permute-start(f32[9,5376]{1,0:T(8,128)} %squeeze.221), channel_id=1, source_target_pairs={{124,0},{125,1},{126,2},{127,3},{0,4},{1,5},{2,6},{3,7},{4,8},{5,9... | collective-permute-start | bytes 580616 | tf_op jit(solution)/shard_map/ppermute | solution.py:15
  218.8 352.0 %collective-permute-start.1 = (f32[9,5376]{1,0:T(8,128)}, f32[9,5376]{1,0:T(8,128)}, u32[]{:S(2)}, u32[]{:S(2)}) collective-permute-start(f32[9,5376]{1,0:T(8,128)} %squeeze.222), channel_id=1, source_target_pairs={{125,0},{126,1},{127,2},{0,3},{1,4},{2,5},{3,6},{4,7},{5,8},{6,9},... | collective-permute-start | bytes 580616 | tf_op jit(solution)/shard_map/ppermute | solution.py:15
  223.8 349.1 %collective-permute-start.2 = (f32[9,5376]{1,0:T(8,128)}, f32[9,5376]{1,0:T(8,128)}, u32[]{:S(2)}, u32[]{:S(2)}) collective-permute-start(f32[9,5376]{1,0:T(8,128)} %squeeze.223), channel_id=1, source_target_pairs={{126,0},{127,1},{0,2},{1,3},{2,4},{3,5},{4,6},{5,7},{6,8},{7,9},{8... | collective-permute-start | bytes 580616 | tf_op jit(solution)/shard_map/ppermute | solution.py:15
  229.3 351.6 %collective-permute-start.3 = (f32[9,5376]{1,0:T(8,128)}, f32[9,5376]{1,0:T(8,128)}, u32[]{:S(2)}, u32[]{:S(2)}) collective-permute-start(f32[9,5376]{1,0:T(8,128)} %squeeze.224), channel_id=1, source_target_pairs={{127,0},{0,1},{1,2},{2,3},{3,4},{4,5},{5,6},{6,7},{7,8},{8,9},{9,1... | collective-permute-start | bytes 580616 | tf_op jit(solution)/shard_map/ppermute | solution.py:15
  233.2 349.5 %collective-permute-start.4 = (f32[9,5376]{1,0:T(8,128)}, f32[9,5376]{1,0:T(8,128)}, u32[]{:S(2)}, u32[]{:S(2)}) collective-permute-start(f32[9,5376]{1,0:T(8,128)} %squeeze.225), channel_id=1, source_target_pairs={{1,0},{2,1},{3,2},{4,3},{5,4},{6,5},{7,6},{8,7},{9,8},{10,9},{11,1... | collective-permute-start | bytes 580616 | tf_op jit(solution)/shard_map/ppermute | solution.py:15
  566.5 18.1 %collective-permute-start.5 = (f32[9,5376]{1,0:T(8,128)}, f32[9,5376]{1,0:T(8,128)S(1)}, u32[]{:S(2)}, u32[]{:S(2)}) collective-permute-start(f32[9,5376]{1,0:T(8,128)} %squeeze.226), channel_id=1, source_target_pairs={{2,0},{3,1},{4,2},{5,3},{6,4},{7,5},{8,6},{9,7},{10,8},{11,9},{12,... | collective-permute-start | bytes 580616 | tf_op jit(solution)/shard_map/ppermute | solution.py:15
  570.7 18.0 %collective-permute-start.6 = (f32[9,5376]{1,0:T(8,128)}, f32[9,5376]{1,0:T(8,128)S(1)}, u32[]{:S(2)}, u32[]{:S(2)}) collective-permute-start(f32[9,5376]{1,0:T(8,128)} %squeeze.227), channel_id=1, source_target_pairs={{3,0},{4,1},{5,2},{6,3},{7,4},{8,5},{9,6},{10,7},{11,8},{12,9},{13... | collective-permute-start | bytes 580616 | tf_op jit(solution)/shard_map/ppermute | solution.py:15
  572.9 23.1 %collective-permute-start.7 = (f32[9,5376]{1,0:T(8,128)S(1)}, f32[9,5376]{1,0:T(8,128)S(1)}, u32[]{:S(2)}, u32[]{:S(2)}) collective-permute-start(f32[9,5376]{1,0:T(8,128)S(1)} %copy-done.114), channel_id=1, source_target_pairs={{4,0},{5,1},{6,2},{7,3},{8,4},{9,5},{10,6},{11,7},{12,8},{13,9},{1... | collective-permute-start | bytes 580616 | tf_op jit(solution)/shard_map/ppermute | solution.py:15
  743.4 19.1 %collective-permute-start.9 = (f32[9,5376]{1,0:T(8,128)}, f32[9,5376]{1,0:T(8,128)S(1)}, u32[]{:S(2)}, u32[]{:S(2)}) collective-permute-start(f32[9,5376]{1,0:T(8,128)} %squeeze.246), channel_id=1, source_target_pairs={{125,0},{126,1},{127,2},{0,3},{1,4},{2,5},{3,6},{4,7},{5,8},{6,9},... | collective-permute-start | bytes 580616 | tf_op jit(solution)/shard_map/ppermute | solution.py:15
  745.5 19.8 %collective-permute-start.10 = (f32[9,5376]{1,0:T(8,128)}, f32[9,5376]{1,0:T(8,128)S(1)}, u32[]{:S(2)}, u32[]{:S(2)}) collective-permute-start(f32[9,5376]{1,0:T(8,128)} %squeeze.247), channel_id=1, source_target_pairs={{126,0},{127,1},{0,2},{1,3},{2,4},{3,5},{4,6},{5,7},{6,8},{7,9},{8... | collective-permute-start | bytes 580616 | tf_op jit(solution)/shard_map/ppermute | solution.py:15
  745.5 31.9 %collective-permute-start.11 = (f32[9,5376]{1,0:T(8,128)}, f32[9,5376]{1,0:T(8,128)}, u32[]{:S(2)}, u32[]{:S(2)}) collective-permute-start(f32[9,5376]{1,0:T(8,128)} %squeeze.248), channel_id=1, source_target_pairs={{127,0},{0,1},{1,2},{2,3},{3,4},{4,5},{5,6},{6,7},{7,8},{8,9},{9,1... | collective-permute-start | bytes 580616 | tf_op jit(solution)/shard_map/ppermute | solution.py:15
  745.5 33.7 %collective-permute-start.12 = (f32[9,5376]{1,0:T(8,128)}, f32[9,5376]{1,0:T(8,128)}, u32[]{:S(2)}, u32[]{:S(2)}) collective-permute-start(f32[9,5376]{1,0:T(8,128)} %squeeze.249), channel_id=1, source_target_pairs={{1,0},{2,1},{3,2},{4,3},{5,4},{6,5},{7,6},{8,7},{9,8},{10,9},{11,1... | collective-permute-start | bytes 580616 | tf_op jit(solution)/shard_map/ppermute | solution.py:15
  750.4 30.6 %collective-permute-start.13 = (f32[9,5376]{1,0:T(8,128)}, f32[9,5376]{1,0:T(8,128)}, u32[]{:S(2)}, u32[]{:S(2)}) collective-permute-start(f32[9,5376]{1,0:T(8,128)} %squeeze.250), channel_id=1, source_target_pairs={{2,0},{3,1},{4,2},{5,3},{6,4},{7,5},{8,6},{9,7},{10,8},{11,9},{12,... | collective-permute-start | bytes 580616 | tf_op jit(solution)/shard_map/ppermute | solution.py:15
  762.5 20.4 %collective-permute-start.14 = (f32[9,5376]{1,0:T(8,128)}, f32[9,5376]{1,0:T(8,128)}, u32[]{:S(2)}, u32[]{:S(2)}) collective-permute-start(f32[9,5376]{1,0:T(8,128)} %squeeze.251), channel_id=1, source_target_pairs={{3,0},{4,1},{5,2},{6,3},{7,4},{8,5},{9,6},{10,7},{11,8},{12,9},{13... | collective-permute-start | bytes 580616 | tf_op jit(solution)/shard_map/ppermute | solution.py:15
  765.3 19.4 %collective-permute-start.15 = (f32[9,5376]{1,0:T(8,128)}, f32[9,5376]{1,0:T(8,128)}, u32[]{:S(2)}, u32[]{:S(2)}) collective-permute-start(f32[9,5376]{1,0:T(8,128)} %squeeze.252), channel_id=1, source_target_pairs={{4,0},{5,1},{6,2},{7,3},{8,4},{9,5},{10,6},{11,7},{12,8},{13,9},{1... | collective-permute-start | bytes 580616 | tf_op jit(solution)/shard_map/ppermute | solution.py:15
  1001.7 28.1 %collective-permute-start.17 = (f32[9,5376]{1,0:T(8,128)}, f32[9,5376]{1,0:T(8,128)S(1)}, u32[]{:S(2)}, u32[]{:S(2)}) collective-permute-start(f32[9,5376]{1,0:T(8,128)} %squeeze.270), channel_id=1, source_target_pairs={{125,0},{126,1},{127,2},{0,3},{1,4},{2,5},{3,6},{4,7},{5,8},{6,9},... | collective-permute-start | bytes 580616 | tf_op jit(solution)/shard_map/ppermute | solution.py:15
  1014.3 20.4 %collective-permute-start.18 = (f32[9,5376]{1,0:T(8,128)}, f32[9,5376]{1,0:T(8,128)S(1)}, u32[]{:S(2)}, u32[]{:S(2)}) collective-permute-start(f32[9,5376]{1,0:T(8,128)} %squeeze.271), channel_id=1, source_target_pairs={{126,0},{127,1},{0,2},{1,3},{2,4},{3,5},{4,6},{5,7},{6,8},{7,9},{8... | collective-permute-start | bytes 580616 | tf_op jit(solution)/shard_map/ppermute | solution.py:15
  1014.4 25.9 %collective-permute-start.19 = (f32[9,5376]{1,0:T(8,128)}, f32[9,5376]{1,0:T(8,128)}, u32[]{:S(2)}, u32[]{:S(2)}) collective-permute-start(f32[9,5376]{1,0:T(8,128)} %squeeze.272), channel_id=1, source_target_pairs={{127,0},{0,1},{1,2},{2,3},{3,4},{4,5},{5,6},{6,7},{7,8},{8,9},{9,1... | collective-permute-start | bytes 580616 | tf_op jit(solution)/shard_map/ppermute | solution.py:15
  1014.4 27.7 %collective-permute-start.20 = (f32[9,5376]{1,0:T(8,128)}, f32[9,5376]{1,0:T(8,128)}, u32[]{:S(2)}, u32[]{:S(2)}) collective-permute-start(f32[9,5376]{1,0:T(8,128)} %squeeze.273), channel_id=1, source_target_pairs={{1,0},{2,1},{3,2},{4,3},{5,4},{6,5},{7,6},{8,7},{9,8},{10,9},{11,1... | collective-permute-start | bytes 580616 | tf_op jit(solution)/shard_map/ppermute | solution.py:15
  1016.5 27.4 %collective-permute-start.21 = (f32[9,5376]{1,0:T(8,128)}, f32[9,5376]{1,0:T(8,128)}, u32[]{:S(2)}, u32[]{:S(2)}) collective-permute-start(f32[9,5376]{1,0:T(8,128)} %squeeze.274), channel_id=1, source_target_pairs={{2,0},{3,1},{4,2},{5,3},{6,4},{7,5},{8,6},{9,7},{10,8},{11,9},{12,... | collective-permute-start | bytes 580616 | tf_op jit(solution)/shard_map/ppermute | solution.py:15
  1194.4 24.1 %collective-permute-start.25 = (f32[9,5376]{1,0:T(8,128)}, f32[9,5376]{1,0:T(8,128)S(1)}, u32[]{:S(2)}, u32[]{:S(2)}) collective-permute-start(f32[9,5376]{1,0:T(8,128)} %squeeze.282), channel_id=1, source_target_pairs={{125,0},{126,1},{127,2},{0,3},{1,4},{2,5},{3,6},{4,7},{5,8},{6,9},... | collective-permute-start | bytes 580616 | tf_op jit(solution)/shard_map/ppermute | solution.py:15
  1203.4 25.9 %collective-permute-start.27 = (f32[9,5376]{1,0:T(8,128)}, f32[9,5376]{1,0:T(8,128)}, u32[]{:S(2)}, u32[]{:S(2)}) collective-permute-start(f32[9,5376]{1,0:T(8,128)} %squeeze.284), channel_id=1, source_target_pairs={{127,0},{0,1},{1,2},{2,3},{3,4},{4,5},{5,6},{6,7},{7,8},{8,9},{9,1... | collective-permute-start | bytes 580616 | tf_op jit(solution)/shard_map/ppermute | solution.py:15
  1203.5 27.7 %collective-permute-start.28 = (f32[9,5376]{1,0:T(8,128)}, f32[9,5376]{1,0:T(8,128)}, u32[]{:S(2)}, u32[]{:S(2)}) collective-permute-start(f32[9,5376]{1,0:T(8,128)} %squeeze.285), channel_id=1, source_target_pairs={{1,0},{2,1},{3,2},{4,3},{5,4},{6,5},{7,6},{8,7},{9,8},{10,9},{11,1... | collective-permute-start | bytes 580616 | tf_op jit(solution)/shard_map/ppermute | solution.py:15
  1204.9 28.1 %collective-permute-start.29 = (f32[9,5376]{1,0:T(8,128)}, f32[9,5376]{1,0:T(8,128)}, u32[]{:S(2)}, u32[]{:S(2)}) collective-permute-start(f32[9,5376]{1,0:T(8,128)} %squeeze.286), channel_id=1, source_target_pairs={{2,0},{3,1},{4,2},{5,3},{6,4},{7,5},{8,6},{9,7},{10,8},{11,9},{12,... | collective-permute-start | bytes 580616 | tf_op jit(solution)/shard_map/ppermute | solution.py:15
  (470 other events, 12096.4 us)
